TPU v7x, 32 devices: a whole 2x2x4 slice. The times are simulated.
32 devices in a mesh: dp: 4 (over z), ctx: 8 (over y, x, core).
Axes of the slice: x: 2, y: 2, z: 4, core: 2. Of those that a mesh axis runs over, the one named last changes fastest.
Arguments:
- inputs: bfloat16 [4, 2048, 4096], P('dp', 'ctx'), may hold values from -6 to 6
- value_weight: bfloat16 [4096, 512], P('ctx'), may hold values from -0.09375 to 0.09375
- query_states: bfloat16 [4, 2048, 2048], P('dp', 'ctx'), may hold values from -40 to 40
- key_states: bfloat16 [4, 2048, 512], P('dp', 'ctx'), may hold values from -6 to 6
- value_states: bfloat16 [4, 2048, 512], P('dp', 'ctx'), may hold values from -6 to 6
- attention_out: bfloat16 [4, 2048, 2048], P('dp', 'ctx'), may hold values from -4 to 4
- out_grad: bfloat16 [4, 2048, 2048], P('dp', 'ctx'), may hold values from -6 to 6
- segment_ids: int32 [4, 2048], P('dp', 'ctx'), may hold values from 0 to 3, never falling along the last dimension, each value on 1 to 1024 neighbouring positions
Outputs:
- query_grad: bfloat16 [4, 2048, 2048], P('dp', 'ctx')
- key_grad: bfloat16 [4, 2048, 512], P('dp', 'ctx')
- input_grad: bfloat16 [4, 2048, 4096], P('dp', 'ctx')
- weight_grad: float32 [4096, 512], P('ctx')
Inputs may be any that keep to these rules, and one draw needn't show every extreme that they name: `segment_ids`: along each sequence the ids never fall; each record holds 1 to 1024 tokens and one holds exactly 1024.
All inputs are finite; a program needn't handle non-finite values.
Results may differ from a plain program's by a relative error of at most 0.0057.
Values may be sent and summed in bfloat16 or wider, within the bound.
No kernel may reach another device: no remote copies, remote signals or barrier semaphores. Data moves between devices by JAX's collectives and lax.ppermute only.
A program may use at most 128 MiB of HBM per device.

v0:
```python
import math
import jax
import jax.numpy as jnp
from jax import lax
from jax.sharding import PartitionSpec as P

HQ = 16
KVH = 4
DH = 128
W = 2048


def carried_in(value, axis, combine, identity):
    peers, here = (lax.axis_size(axis), lax.axis_index(axis))
    everything = jax.tree.map(lambda part: lax.all_gather(part, axis), value)
    start = jax.tree.map(
        lambda part, zero: jnp.broadcast_to(jnp.asarray(zero, part.dtype), part.shape),
        value,
        identity,
    )

    def turn(k, before):
        reached = k < here
        new = combine(before, jax.tree.map(lambda part: part[k], everything))
        return jax.tree.map(lambda a, b: jnp.where(reached, a, b), new, before)

    return lax.fori_loop(0, peers, turn, start)


def passed_along(block, axis, distance):
    devices = range(lax.axis_size(axis))
    route = [(i - distance, i) for i in devices if i - distance in devices]
    return lax.ppermute(block, axis, route)


def link_records(earlier, later):
    first_early, last_early, start_early, whole_early, empty_early = earlier
    first_late, last_late, start_late, whole_late, empty_late = later
    joined = last_early == first_late
    start_merged = jnp.where((whole_late == 1) & joined, start_early, start_late)
    whole_merged = jnp.where((whole_early == 1) & (whole_late == 1) & joined, 1, 0).astype(
        jnp.int32
    )
    merged = (first_early, last_late, start_merged, whole_merged, jnp.zeros_like(empty_early))
    return tuple(
        (
            jnp.where(
                empty_early == 1, late_item, jnp.where(empty_late == 1, early_item, merged_item)
            )
            for early_item, late_item, merged_item in zip(earlier, later, merged)
        )
    )


def attend_group(operands, live_mask, factor):
    query_group, key_group, value_group, grad_group, output_group = operands
    scores = (
        jnp.einsum("gqd,kd->gqk", query_group, key_group, preferred_element_type=jnp.float32)
        * factor
    )
    scores = jnp.where(live_mask[None], scores, -1e30)
    row_max = jnp.max(scores, axis=-1, keepdims=True)
    exp_score = jnp.exp(scores - row_max)
    prob_full = exp_score / jnp.sum(exp_score, axis=-1, keepdims=True)
    prob_low = prob_full.astype(jnp.bfloat16)
    row_delta = jnp.sum(
        grad_group.astype(jnp.float32) * output_group.astype(jnp.float32), axis=-1, keepdims=True
    )
    prob_grad = jnp.einsum(
        "gqd,kd->gqk", grad_group, value_group, preferred_element_type=jnp.float32
    )
    score_grad = (prob_full * (prob_grad - row_delta)).astype(jnp.bfloat16)
    query_part = (
        jnp.einsum("gqk,kd->gqd", score_grad, key_group, preferred_element_type=jnp.float32)
        * factor
    )
    key_part = (
        jnp.einsum("gqk,gqd->kd", score_grad, query_group, preferred_element_type=jnp.float32)
        * factor
    )
    value_part = jnp.einsum("gqk,gqd->kd", prob_low, grad_group, preferred_element_type=jnp.float32)
    return (query_part, key_part, value_part)


def attend_tail(factor, operands):
    query_heads, key_heads, value_heads, grad_heads, output_heads, live_mask = operands
    query_part, key_part, value_part = lax.map(
        lambda head_parts: attend_group(head_parts, live_mask, factor),
        (query_heads, key_heads, value_heads, grad_heads, output_heads),
    )
    return (query_part, key_part, value_part)


def on_device(
    inputs,
    value_weight,
    query_states,
    key_states,
    value_states,
    attention_out,
    out_grad,
    segment_ids,
):
    tok_rows = query_states.shape[1]
    span_blocks = W // tok_rows
    group_size = HQ // KVH
    width_kv = KVH * DH
    factor = 1.0 / math.sqrt(DH)
    window_rows = (span_blocks + 1) * tok_rows
    input_rows = inputs[0]
    values = value_states[0]
    seg_local = segment_ids[0]
    device_index = lax.axis_index("ctx")
    offset = device_index * tok_rows
    before = jnp.sum((seg_local[None, :] < seg_local[:, None]).astype(jnp.int32), axis=1)
    first_id = seg_local[0]
    last_id = seg_local[-1]
    summary = (
        first_id,
        last_id,
        offset + before[-1],
        (first_id == last_id).astype(jnp.int32),
        jnp.zeros((), jnp.int32),
    )
    identity = tuple((jnp.full((), filler, jnp.int32) for filler in (0, 0, 0, 1, 1)))
    prior = carried_in(summary, "ctx", link_records, identity)
    carried = (before == 0) & (prior[4] == 0) & (prior[1] == first_id)
    starts = jnp.where(carried, prior[2], offset + before)
    kv_block = jnp.stack([key_states[0], values])
    doubling_plan = []
    window = kv_block
    blocks_held = 1
    while blocks_held < span_blocks + 1:
        needed = min(blocks_held, span_blocks + 1 - blocks_held)
        received = passed_along(window[:, (blocks_held - needed) * tok_rows :], "ctx", blocks_held)
        window = jnp.concatenate([received, window], axis=1)
        doubling_plan.append((blocks_held, needed))
        blocks_held = blocks_held + needed
    key_base = offset - span_blocks * tok_rows
    key_pos = key_base + jnp.arange(window_rows, dtype=jnp.int32)
    query_pos = offset + jnp.arange(tok_rows, dtype=jnp.int32)
    live_mask = (
        (key_pos[None, :] >= starts[:, None])
        & (key_pos[None, :] <= query_pos[:, None])
        & (key_pos[None, :] > query_pos[:, None] - W)
    )
    query_heads = query_states[0].reshape(tok_rows, KVH, group_size, DH).transpose(1, 2, 0, 3)
    grad_heads = out_grad[0].reshape(tok_rows, KVH, group_size, DH).transpose(1, 2, 0, 3)
    output_heads = attention_out[0].reshape(tok_rows, KVH, group_size, DH).transpose(1, 2, 0, 3)
    key_heads = window[0].reshape(window_rows, KVH, DH).transpose(1, 0, 2)
    value_heads = window[1].reshape(window_rows, KVH, DH).transpose(1, 0, 2)
    operands = (query_heads, key_heads, value_heads, grad_heads, output_heads, live_mask)
    query_part, key_part, value_part = attend_tail(factor, operands)
    query_grad = query_part.transpose(2, 0, 1, 3).reshape(1, tok_rows, HQ * DH).astype(jnp.bfloat16)
    grads = jnp.stack(
        [
            key_part.transpose(1, 0, 2).reshape(window_rows, width_kv),
            value_part.transpose(1, 0, 2).reshape(window_rows, width_kv),
        ]
    )
    for blocks_held, needed in reversed(doubling_plan):
        sent = grads[:, : needed * tok_rows]
        kept_rows = grads[:, needed * tok_rows :]
        returned = passed_along(sent, "ctx", -blocks_held)
        split_at = (blocks_held - needed) * tok_rows
        grads = jnp.concatenate(
            [kept_rows[:, :split_at], kept_rows[:, split_at:] + returned], axis=1
        )
    key_grad = grads[0].astype(jnp.bfloat16)[None]
    value_delta = grads[1].astype(jnp.bfloat16)
    input_grad = jnp.einsum(
        "tk,rk->tr",
        value_delta,
        lax.all_gather(value_weight, "ctx", axis=0, tiled=True),
        preferred_element_type=jnp.float32,
    )
    input_grad = input_grad.astype(jnp.bfloat16)[None]
    weight_share = lax.psum_scatter(
        jnp.einsum("tr,tk->rk", input_rows, value_delta, preferred_element_type=jnp.float32),
        "ctx",
        scatter_dimension=0,
        tiled=True,
    )
    weight_grad = lax.psum(weight_share, "dp")
    return (query_grad, key_grad, input_grad, weight_grad)


def solution(mesh):
    placed = (
        P("dp", "ctx", None),
        P("ctx", None),
        P("dp", "ctx", None),
        P("dp", "ctx", None),
        P("dp", "ctx", None),
        P("dp", "ctx", None),
        P("dp", "ctx", None),
        P("dp", "ctx"),
    )
    return jax.shard_map(
        on_device,
        mesh=mesh,
        in_specs=placed,
        out_specs=(
            P("dp", "ctx", None),
            P("dp", "ctx", None),
            P("dp", "ctx", None),
            P("ctx", None),
        ),
        check_vma=False,
    )
```

profile of v0, /device:TPU:0, one launch (start us, length us, event | category | flops | bytes accessed | tf_op | source)
XLA Modules:
  0.0 681.1 jit_solution(11382272146703181672)
XLA Ops:
  14.6 11.5 %collective-permute-start.2 = (bf16[2,512,512]{1,2,0:T(8,128)(2,1)S(1)}, bf16[2,512,512]{1,2,0:T(8,128)(2,1)S(1)}, u32[]{:S(2)}, u32[]{:S(2)}) collective-permute-start(bf16[2,512,512]{1,2,0:T(8,128)(2,1)S(1)} %maximum_maximum_fusion.1), channel_id=1, source_target_pairs={{0,2},{1,3},{2,4},{3,5},{4,6},{5,7},{8,10},{9,11},{10,12},{11,13},... | collective-permute-start | bytes 3145736 | tf_op jit(solution)/shard_map/ppermute | solution.py:33
  26.1 21.7 %collective-permute-done.2 = bf16[2,512,512]{1,2,0:T(8,128)(2,1)S(1)} collective-permute-done((bf16[2,512,512]{1,2,0:T(8,128)(2,1)S(1)}, bf16[2,512,512]{1,2,0:T(8,128)(2,1)S(1)}, u32[]{:S(2)}, u32[]{:S(2)}) %collective-permute-start.2) | collective-permute-done | bytes 1048608 | tf_op jit(solution)/shard_map/ppermute | solution.py:33
  50.5 6.7 collective-permute-start.3
  67.4 31.2 %all-reduce.5 = (s32[8]{0:T(128)S(1)}, s32[8]{0:T(128)S(1)}, s32[8]{0:T(128)S(1)}, s32[8]{0:T(128)S(1)}, s32[8]{0:T(128)S(1)}) all-reduce(s32[8]{0:T(128)S(1)} %bitcast_dynamic-update-slice_fusion.1, s32[8]{0:T(128)S(1)} %dynamic-update-slice.1, s32[8]{0:T(128)S(1)} %dynamic-update-slice.2, ...), channel_id=2, replica_groups=mesh['dp'=4,'ctx'=8] {'ctx'}, use_global_device_ids=true, to_apply=%add | all-reduce | flops 40 | bytes 320 | tf_op jit(solution)/shard_map/all_gather | solution.py:15
  98.6 66.3 %while.32 = (s32[]{:T(128)}, s32[]{:T(128)}, s32[]{:T(128)}, s32[]{:T(128)}, s32[]{:T(128)}, /*index=5*/s32[8]{0:T(128)S(1)}, s32[8]{0:T(128)S(1)}, s32[8]{0:T(1...) while((s32[]{:T(128)}, s32[]{:T(128)}, s32[]{:T(128)}, s32[]{:T(128)}, ...), condition=%wide.region_2.3_spmd, body=%wide.region_1.2_spmd.sunk | while | flops 18 | bytes 363 | solution.py:27
  178.1 120.7 %while.33 = (s32[]{:T(128)}, bf16[4,4,256,128]{3,2,1,0:T(8,128)(2,1)}, f32[4,2304,128]{2,1,0:T(8,128)}, f32[4,2304,128]{2,1,0:T(8,128)}, bf16[4,4,256,128]{2,3,1...) while((s32[]{:T(128)}, ...), condition=%wide.region_7.8_spmd.clone, body=%wide.region_3.7_spmd.clone.sunk | while | flops 3658453504 | bytes 52402368 | solution.py:87
  180.5 8.4 %fusion.118 = (f32[4,256]{1,0:T(4,128)S(1)}, f32[4,256,2304]{2,1,0:T(8,128)}) fusion(pred[256,2304]{1,0:T(8,128)(4,1)S(1)} %compare_and_fusion.2, bf16[4,2304,128]{1,2,0:T(8,128)(2,1)} %get-tuple-element.586, s32[]{:T(128)} %get-tuple-element.567, bf16[4,4,256,128]{2,3,1,0:T(8,128)(2,1)} %get-tuple-element.585), kind=kOutput, calls=%fused_computation.87.clone.1 | convolution fusion | flops 613419264 | bytes 10884096 | tf_op jit(solution)/shard_map/while/body/eval_jaxpr/sub | solution.py:63
  201.4 6.8 fusion.121
  210.7 8.4 %fusion.118 = (f32[4,256]{1,0:T(4,128)S(1)}, f32[4,256,2304]{2,1,0:T(8,128)}) fusion(pred[256,2304]{1,0:T(8,128)(4,1)S(1)} %compare_and_fusion.2, bf16[4,2304,128]{1,2,0:T(8,128)(2,1)} %get-tuple-element.586, s32[]{:T(128)} %get-tuple-element.567, bf16[4,4,256,128]{2,3,1,0:T(8,128)(2,1)} %get-tuple-element.585), kind=kOutput, calls=%fused_computation.87.clone.1 | convolution fusion | flops 613419264 | bytes 10884096 | tf_op jit(solution)/shard_map/while/body/eval_jaxpr/sub | solution.py:63
  231.5 6.8 %fusion.121 = f32[4,2304,128]{2,1,0:T(8,128)} fusion(f32[4,2304,128]{2,1,0:T(8,128)} %get-tuple-element.570, s32[]{:T(128)} %get-tuple-element.567, f32[4,256]{1,0:T(4,128)S(1)} %get-tuple-element.513, pred[256,2304]{1,0:T(8,128)(4,1)S(1)} %compare_and_fusion.2, bf16[4,2304,128]{1,2,0:T(8,128)(2,1)} %get-tuple-element.586, ...), kind=kOutput, calls=%fused_computation.17.clone.1 | convolution fusion | flops 1219759360 | bytes 2889728 | tf_op jit(solution)/shard_map/while/body/eval_jaxpr/gqk,gqd->kd/dot_general | solution.py:81
  240.8 8.4 %fusion.118 = (f32[4,256]{1,0:T(4,128)S(1)}, f32[4,256,2304]{2,1,0:T(8,128)}) fusion(pred[256,2304]{1,0:T(8,128)(4,1)S(1)} %compare_and_fusion.2, bf16[4,2304,128]{1,2,0:T(8,128)(2,1)} %get-tuple-element.586, s32[]{:T(128)} %get-tuple-element.567, bf16[4,4,256,128]{2,3,1,0:T(8,128)(2,1)} %get-tuple-element.585), kind=kOutput, calls=%fused_computation.87.clone.1 | convolution fusion | flops 613419264 | bytes 10884096 | tf_op jit(solution)/shard_map/while/body/eval_jaxpr/sub | solution.py:63
  261.8 6.8 fusion.121
  271.0 8.4 %fusion.118 = (f32[4,256]{1,0:T(4,128)S(1)}, f32[4,256,2304]{2,1,0:T(8,128)}) fusion(pred[256,2304]{1,0:T(8,128)(4,1)S(1)} %compare_and_fusion.2, bf16[4,2304,128]{1,2,0:T(8,128)(2,1)} %get-tuple-element.586, s32[]{:T(128)} %get-tuple-element.567, bf16[4,4,256,128]{2,3,1,0:T(8,128)(2,1)} %get-tuple-element.585), kind=kOutput, calls=%fused_computation.87.clone.1 | convolution fusion | flops 613419264 | bytes 10884096 | tf_op jit(solution)/shard_map/while/body/eval_jaxpr/sub | solution.py:63
  279.4 5.4 multiply_convert_fusion.2
  291.9 6.8 %fusion.121 = f32[4,2304,128]{2,1,0:T(8,128)} fusion(f32[4,2304,128]{2,1,0:T(8,128)} %get-tuple-element.570, s32[]{:T(128)} %get-tuple-element.567, f32[4,256]{1,0:T(4,128)S(1)} %get-tuple-element.513, pred[256,2304]{1,0:T(8,128)(4,1)S(1)} %compare_and_fusion.2, bf16[4,2304,128]{1,2,0:T(8,128)(2,1)} %get-tuple-element.586, ...), kind=kOutput, calls=%fused_computation.17.clone.1 | convolution fusion | flops 1219759360 | bytes 2889728 | tf_op jit(solution)/shard_map/while/body/eval_jaxpr/gqk,gqd->kd/dot_general | solution.py:81
  298.7 11.1 %copy.47 = f32[2304,4,128]{2,1,0:T(4,128)} copy(f32[2304,4,128]{2,0,1:T(8,128)} %bitcast.169) | data formatting | bytes 9437184 | tf_op jit(solution)/shard_map/transpose | solution.py:157
  309.8 6.6 stack_reshape.6
  321.6 10.9 %copy.48 = f32[2304,4,128]{2,1,0:T(4,128)} copy(f32[2304,4,128]{2,0,1:T(8,128)S(1)} %bitcast.172) | data formatting | bytes 9437184 | tf_op jit(solution)/shard_map/transpose | solution.py:158
  332.5 6.5 stack_reshape.7
  351.8 86.6 %collective-permute-done.5 = f32[2,1024,512]{2,1,0:T(8,128)} collective-permute-done((f32[2,1024,512]{2,1,0:T(8,128)S(1)}, f32[2,1024,512]{2,1,0:T(8,128)}, u32[]{:S(2)}, u32[]{:S(2)}) %collective-permute-start.5) | collective-permute-done | bytes 4194336 | tf_op jit(solution)/shard_map/ppermute | solution.py:33
  443.1 43.9 %collective-permute-done.6 = f32[2,512,512]{2,1,0:T(8,128)S(1)} collective-permute-done((f32[2,512,512]{2,1,0:T(8,128)S(1)}, f32[2,512,512]{2,1,0:T(8,128)S(1)}, u32[]{:S(2)}, u32[]{:S(2)}) %collective-permute-start.6) | collective-permute-done | bytes 2097184 | tf_op jit(solution)/shard_map/ppermute | solution.py:33
  498.6 80.7 %reduce-scatter.2.cloned.1.call-done = f32[512,512]{0,1:T(8,128)} async-done(((f32[4096,512]{0,1:T(8,128)}), f32[512,512]{0,1:T(8,128)}) %reduce-scatter.2.cloned.1.call-update) | async-done | bytes 1048592 | tf_op jit(solution)/shard_map/reduce_scatter | solution.py:178
  584.6 33.2 %all-gather.4.cloned.1.call-done = bf16[4096,512]{1,0:T(8,128)(2,1)} async-done(((bf16[512,512]{1,0:T(8,128)(2,1)}), bf16[4096,512]{1,0:T(8,128)(2,1)}) %all-gather.4.cloned.1.call-update) | async-done | bytes 4194320 | tf_op jit(solution)/shard_map/all_gather | solution.py:174
  622.7 49.4 %all-reduce.8.cloned.1.call-done = f32[512,512]{0,1:T(8,128)} async-done(((f32[512,512]{0,1:T(8,128)}), f32[512,512]{0,1:T(8,128)}) %all-reduce.8.cloned.1.call-update) | async-done | bytes 1048592 | tf_op jit(solution)/shard_map/psum | solution.py:184
  (174 shorter events, 157.3 us)
Async XLA Ops:
  7.2 486.1 %copy-start = (bf16[1,256,4096]{2,1,0:T(8,128)(2,1)S(1)}, bf16[1,256,4096]{2,1,0:T(8,128)(2,1)}, u32[]{:S(2)}) copy-start(bf16[1,256,4096]{2,1,0:T(8,128)(2,1)} %param.12) | copy-start | bytes 6291460
  7.2 54.1 %copy-start.8 = (u32[32]{0:T(128)S(1)}, u32[32]{0:T(128)}, u32[]{:S(2)}) copy-start(u32[32]{0:T(128)} %constant.81) | copy-start | bytes 388
  7.2 51.4 %copy-start.7 = (s32[1,256]{1,0:T(1,128)S(1)}, s32[1,256]{1,0:T(1,128)}, u32[]{:S(2)}) copy-start(s32[1,256]{1,0:T(1,128)} %param.19) | copy-start | bytes 3076
  7.2 572.1 %reduce-scatter.2.cloned.1.call-start = ((), (), s32[]{:S(2)}) async-start(), calls=%async_computation.2 | async-start | bytes 9437184 | tf_op jit(solution)/shard_map/reduce_scatter | solution.py:178
  10.4 4.1 collective-permute-start.1
  14.6 33.3 %collective-permute-start.2 = (bf16[2,512,512]{1,2,0:T(8,128)(2,1)S(1)}, bf16[2,512,512]{1,2,0:T(8,128)(2,1)S(1)}, u32[]{:S(2)}, u32[]{:S(2)}) collective-permute-start(bf16[2,512,512]{1,2,0:T(8,128)(2,1)S(1)} %maximum_maximum_fusion.1), channel_id=1, source_target_pairs={{0,2},{1,3},{2,4},{3,5},{4,6},{5,7},{8,10},{9,11},{10,12},{11,13},... | collective-permute-start | bytes 3145736 | tf_op jit(solution)/shard_map/ppermute | solution.py:33
  50.5 123.1 %collective-permute-start.3 = (bf16[2,1024,512]{1,2,0:T(8,128)(2,1)}, bf16[2,1024,512]{1,2,0:T(8,128)(2,1)}, u32[]{:S(2)}, u32[]{:S(2)}) collective-permute-start(bf16[2,1024,512]{1,2,0:T(8,128)(2,1)} %maximum_maximum_fusion), channel_id=1, source_target_pairs={{0,4},{1,5},{2,6},{3,7},{8,12},{9,13},{10,14},{11,15},{16,20},{17,... | collective-permute-start | bytes 6291464 | tf_op jit(solution)/shard_map/ppermute | solution.py:33
  57.1 115.3 %collective-permute-start = (bf16[2,256,512]{1,2,0:T(8,128)(2,1)}, bf16[2,256,512]{1,2,0:T(8,128)(2,1)}, u32[]{:S(2)}, u32[]{:S(2)}) collective-permute-start(bf16[2,256,512]{1,2,0:T(8,128)(2,1)} %pad_maximum_fusion.1), channel_id=1, source_target_pairs={} | collective-permute-start | bytes 1572872 | tf_op jit(solution)/shard_map/ppermute | solution.py:33
  172.4 3.0 copy-start.3
  194.4 3.5 copy-start.5
  200.4 1.0 copy-start.6
  224.5 3.5 copy-start.5
  230.6 1.0 copy-start.6
  254.7 3.6 copy-start.5
  284.8 3.5 copy-start.5
  309.8 11.8 %slice-start = ((s8[4718592]{0:T(1024)(128)(4,1)}), s8[524288]{0:T(1024)(128)(4,1)S(1)}, s32[]{:S(2)}) async-start(s8[4718592]{0:T(1024)(128)(4,1)} %bitcast.170), calls=%async_computation.4 | async-start | bytes 1048576
  316.4 5.2 slice-start.1
  344.1 6.7 copy-start.1
  346.9 91.5 %collective-permute-start.5 = (f32[2,1024,512]{2,1,0:T(8,128)S(1)}, f32[2,1024,512]{2,1,0:T(8,128)}, u32[]{:S(2)}, u32[]{:S(2)}) collective-permute-start(f32[2,1024,512]{2,1,0:T(8,128)S(1)} %slice.82), channel_id=1, source_target_pairs={{4,0},{5,1},{6,2},{7,3},{12,8},{13,9},{14,10},{15,11},{20,16},{21,... | collective-permute-start | bytes 12582920 | tf_op jit(solution)/shard_map/ppermute | solution.py:33
  349.8 1.9 collective-permute-start.4
  441.8 45.2 %collective-permute-start.6 = (f32[2,512,512]{2,1,0:T(8,128)S(1)}, f32[2,512,512]{2,1,0:T(8,128)S(1)}, u32[]{:S(2)}, u32[]{:S(2)}) collective-permute-start(f32[2,512,512]{2,1,0:T(8,128)S(1)} %slice.84), channel_id=1, source_target_pairs={{2,0},{3,1},{4,2},{5,3},{6,4},{7,5},{10,8},{11,9},{12,10},{13,11},... | collective-permute-start | bytes 6291464 | tf_op jit(solution)/shard_map/ppermute | solution.py:33
  487.6 4.6 collective-permute-start.7
  497.8 120.0 %all-gather.4.cloned.1.call-start = ((), (), s32[]{:S(2)}) async-start(), calls=%async_computation.1 | async-start | bytes 4718592 | tf_op jit(solution)/shard_map/all_gather | solution.py:174
  498.5 173.5 %all-reduce.8.cloned.1.call-start = ((), (), s32[]{:S(2)}) async-start(), calls=%async_computation.3 | async-start | bytes 2097152 | tf_op jit(solution)/shard_map/psum | solution.py:184
  (4 other events, 3.7 us)
Sparse Core Ops, SparseCore 0:
  497.9 81.3 reduce-scatter.1
  581.1 36.5 all-gather.3
  620.1 51.8 all-reduce.7
where the time goes:
time: 683 us; the launch traced here: 681 us
  waiting for transfers between devices  321 us (47%)
  local copies, waits for them, and re-layouts  117 us (17%)
  matrix products  116 us (17%)
  loops' own time  40.9 us (6%)
  blocking collectives  31.2 us (5%)
  starting transfers between devices  27.3 us (4%)
  between operations  16.6 us (2%)
  other arithmetic  11.1 us (2%)
    ppermute x8, waiting for transfers between devices, passed_along(): return lax.ppermute(block, axis, route)  157 us
    reduce_scatter x1, waiting for transfers between devices, on_device(): lax.psum_scatter(jnp.einsum('tr,tk->rk', input_rows, value_delta, preferr...  80.7 us
    psum x1, waiting for transfers between devices, on_device(): weight_grad = lax.psum(weight_share, 'dp')  49.4 us
    another operation x1, loops' own time, carried_in(): return lax.fori_loop(0, peers, turn, start)  40.7 us
    sub x4, matrix products, attend_group(): exp_score = jnp.exp(scores - row_max)  33.5 us
    all_gather x1, waiting for transfers between devices, on_device(): lax.all_gather(value_weight, 'ctx', axis=0, tiled=True)  33.2 us
    all_gather x1, blocking collectives, carried_in(): everything = jax.tree.map(lambda part: lax.all_gather(part, axis), value)  31.2 us
    dot_general x4, matrix products, attend_group(): jnp.einsum('gqk,gqd->kd', prob_low, grad_group, preferred_element_type=jn...  27.2 us
  transfers between devices with their start and end apart: 11, of which 8 were waited for; matrix products, arithmetic and copies ran while one was open for 8% of the time, Pallas kernels for 0%

commit v1 on v0

--- a/solution.py
+++ b/solution.py
@@ -181,7 +181,8 @@
         scatter_dimension=0,
         tiled=True,
     )
-    weight_grad = lax.psum(weight_share, "dp")
+    pieces = lax.all_gather(weight_share, "dp")
+    weight_grad = jnp.sum(pieces, axis=0)
     return (query_grad, key_grad, input_grad, weight_grad)
 
 

time: 683 us -> 725 us (1.061)
  waiting for transfers between devices: 321 us -> 349 us
    all_gather x0 -> x1, waiting for transfers between devices: none -> 77.5 us  [on_device(): pieces = lax.all_gather(weight_share, 'dp')]
    psum x1 -> x0, waiting for transfers between devices: 49.4 us -> none  [on_device(): weight_grad = lax.psum(weight_share, 'dp')]
  transfers between devices with their start and end apart: 11 -> 11, of which waited for: 8 -> 8; matrix products, arithmetic and copies ran while one was open for 8% -> 7% of each run, Pallas kernels for 0% -> 0%
where the time goes in v1:
time: 725 us; the launch traced here: 720 us
  waiting for transfers between devices  349 us (48%)
  local copies, waits for them, and re-layouts  121 us (17%)
  matrix products  116 us (16%)
  loops' own time  41.5 us (6%)
  blocking collectives  31.2 us (4%)
  starting transfers between devices  27.2 us (4%)
  between operations  16.8 us (2%)
  other arithmetic  15.8 us (2%)
    ppermute x8, waiting for transfers between devices, passed_along(): return lax.ppermute(block, axis, route)  157 us
    reduce_scatter x1, waiting for transfers between devices, on_device(): lax.psum_scatter(jnp.einsum('tr,tk->rk', input_rows, value_delta, preferr...  80.6 us
    all_gather x1, waiting for transfers between devices, on_device(): pieces = lax.all_gather(weight_share, 'dp')  77.5 us
    another operation x1, loops' own time, carried_in(): return lax.fori_loop(0, peers, turn, start)  40.7 us
    sub x4, matrix products, attend_group(): exp_score = jnp.exp(scores - row_max)  33.5 us
    all_gather x1, waiting for transfers between devices, on_device(): lax.all_gather(value_weight, 'ctx', axis=0, tiled=True)  33.2 us
    all_gather x1, blocking collectives, carried_in(): everything = jax.tree.map(lambda part: lax.all_gather(part, axis), value)  31.2 us
    dot_general x4, matrix products, attend_group(): jnp.einsum('gqk,gqd->kd', prob_low, grad_group, preferred_element_type=jn...  27.2 us
  transfers between devices with their start and end apart: 11, of which 8 were waited for; matrix products, arithmetic and copies ran while one was open for 7% of the time, Pallas kernels for 0%

profile of v1, /device:TPU:0, one launch (start us, length us, event | category | flops | bytes accessed | tf_op | source)
XLA Modules:
  0.0 719.5 jit_solution(216528119444521224)
XLA Ops:
  14.6 11.5 %collective-permute-start.2 = (bf16[2,512,512]{1,2,0:T(8,128)(2,1)S(1)}, bf16[2,512,512]{1,2,0:T(8,128)(2,1)S(1)}, u32[]{:S(2)}, u32[]{:S(2)}) collective-permute-start(bf16[2,512,512]{1,2,0:T(8,128)(2,1)S(1)} %maximum_maximum_fusion.1), channel_id=1, source_target_pairs={{0,2},{1,3},{2,4},{3,5},{4,6},{5,7},{8,10},{9,11},{10,12},{11,13},... | collective-permute-start | bytes 3145736 | tf_op jit(solution)/shard_map/ppermute | solution.py:33
  26.1 21.7 %collective-permute-done.2 = bf16[2,512,512]{1,2,0:T(8,128)(2,1)S(1)} collective-permute-done((bf16[2,512,512]{1,2,0:T(8,128)(2,1)S(1)}, bf16[2,512,512]{1,2,0:T(8,128)(2,1)S(1)}, u32[]{:S(2)}, u32[]{:S(2)}) %collective-permute-start.2) | collective-permute-done | bytes 1048608 | tf_op jit(solution)/shard_map/ppermute | solution.py:33
  50.5 6.7 collective-permute-start.3
  67.4 31.2 %all-reduce.5 = (s32[8]{0:T(128)S(1)}, s32[8]{0:T(128)S(1)}, s32[8]{0:T(128)S(1)}, s32[8]{0:T(128)S(1)}, s32[8]{0:T(128)S(1)}) all-reduce(s32[8]{0:T(128)S(1)} %bitcast_dynamic-update-slice_fusion.1, s32[8]{0:T(128)S(1)} %dynamic-update-slice.1, s32[8]{0:T(128)S(1)} %dynamic-update-slice.2, ...), channel_id=2, replica_groups=mesh['dp'=4,'ctx'=8] {'ctx'}, use_global_device_ids=true, to_apply=%add | all-reduce | flops 40 | bytes 320 | tf_op jit(solution)/shard_map/all_gather | solution.py:15
  98.6 66.3 %while.32 = (s32[]{:T(128)}, s32[]{:T(128)}, s32[]{:T(128)}, s32[]{:T(128)}, s32[]{:T(128)}, /*index=5*/s32[8]{0:T(128)S(1)}, s32[8]{0:T(128)S(1)}, s32[8]{0:T(1...) while((s32[]{:T(128)}, s32[]{:T(128)}, s32[]{:T(128)}, s32[]{:T(128)}, ...), condition=%wide.region_2.3_spmd, body=%wide.region_1.2_spmd.sunk | while | flops 18 | bytes 363 | solution.py:27
  178.1 121.3 %while.33 = (s32[]{:T(128)}, bf16[4,4,256,128]{3,2,1,0:T(8,128)(2,1)}, f32[4,2304,128]{2,1,0:T(8,128)}, f32[4,2304,128]{2,1,0:T(8,128)}, bf16[4,4,256,128]{2,3,1...) while((s32[]{:T(128)}, ...), condition=%wide.region_7.8_spmd.clone, body=%wide.region_3.7_spmd.clone.sunk | while | flops 3658453504 | bytes 52402368 | solution.py:87
  181.0 8.4 %fusion.118 = (f32[4,256]{1,0:T(4,128)S(1)}, f32[4,256,2304]{2,1,0:T(8,128)}) fusion(pred[256,2304]{1,0:T(8,128)(4,1)S(1)} %compare_and_fusion.2, bf16[4,2304,128]{1,2,0:T(8,128)(2,1)} %get-tuple-element.595, s32[]{:T(128)} %get-tuple-element.576, bf16[4,4,256,128]{2,3,1,0:T(8,128)(2,1)} %get-tuple-element.594), kind=kOutput, calls=%fused_computation.87.clone.1 | convolution fusion | flops 613419264 | bytes 10884096 | tf_op jit(solution)/shard_map/while/body/eval_jaxpr/sub | solution.py:63
  201.9 6.8 fusion.121
  211.1 8.4 %fusion.118 = (f32[4,256]{1,0:T(4,128)S(1)}, f32[4,256,2304]{2,1,0:T(8,128)}) fusion(pred[256,2304]{1,0:T(8,128)(4,1)S(1)} %compare_and_fusion.2, bf16[4,2304,128]{1,2,0:T(8,128)(2,1)} %get-tuple-element.595, s32[]{:T(128)} %get-tuple-element.576, bf16[4,4,256,128]{2,3,1,0:T(8,128)(2,1)} %get-tuple-element.594), kind=kOutput, calls=%fused_computation.87.clone.1 | convolution fusion | flops 613419264 | bytes 10884096 | tf_op jit(solution)/shard_map/while/body/eval_jaxpr/sub | solution.py:63
  232.0 6.8 fusion.121
  241.3 8.4 %fusion.118 = (f32[4,256]{1,0:T(4,128)S(1)}, f32[4,256,2304]{2,1,0:T(8,128)}) fusion(pred[256,2304]{1,0:T(8,128)(4,1)S(1)} %compare_and_fusion.2, bf16[4,2304,128]{1,2,0:T(8,128)(2,1)} %get-tuple-element.595, s32[]{:T(128)} %get-tuple-element.576, bf16[4,4,256,128]{2,3,1,0:T(8,128)(2,1)} %get-tuple-element.594), kind=kOutput, calls=%fused_computation.87.clone.1 | convolution fusion | flops 613419264 | bytes 10884096 | tf_op jit(solution)/shard_map/while/body/eval_jaxpr/sub | solution.py:63
  262.2 6.8 fusion.121
  271.5 8.4 %fusion.118 = (f32[4,256]{1,0:T(4,128)S(1)}, f32[4,256,2304]{2,1,0:T(8,128)}) fusion(pred[256,2304]{1,0:T(8,128)(4,1)S(1)} %compare_and_fusion.2, bf16[4,2304,128]{1,2,0:T(8,128)(2,1)} %get-tuple-element.595, s32[]{:T(128)} %get-tuple-element.576, bf16[4,4,256,128]{2,3,1,0:T(8,128)(2,1)} %get-tuple-element.594), kind=kOutput, calls=%fused_computation.87.clone.1 | convolution fusion | flops 613419264 | bytes 10884096 | tf_op jit(solution)/shard_map/while/body/eval_jaxpr/sub | solution.py:63
  292.3 6.8 fusion.121
  299.3 11.1 %copy.61 = f32[2304,4,128]{2,1,0:T(4,128)} copy(f32[2304,4,128]{2,0,1:T(8,128)} %bitcast.171) | data formatting | bytes 9437184 | tf_op jit(solution)/shard_map/transpose | solution.py:157
  310.5 6.6 stack_reshape.6
  322.2 10.9 %copy.62 = f32[2304,4,128]{2,1,0:T(4,128)} copy(f32[2304,4,128]{2,0,1:T(8,128)S(1)} %bitcast.174) | data formatting | bytes 9437184 | tf_op jit(solution)/shard_map/transpose | solution.py:158
  333.1 6.5 stack_reshape.7
  352.4 86.7 %collective-permute-done.5 = f32[2,1024,512]{2,1,0:T(8,128)} collective-permute-done((f32[2,1024,512]{2,1,0:T(8,128)S(1)}, f32[2,1024,512]{2,1,0:T(8,128)}, u32[]{:S(2)}, u32[]{:S(2)}) %collective-permute-start.5) | collective-permute-done | bytes 4194336 | tf_op jit(solution)/shard_map/ppermute | solution.py:33
  443.8 44.0 %collective-permute-done.6 = f32[2,512,512]{2,1,0:T(8,128)S(1)} collective-permute-done((f32[2,512,512]{2,1,0:T(8,128)S(1)}, f32[2,512,512]{2,1,0:T(8,128)S(1)}, u32[]{:S(2)}, u32[]{:S(2)}) %collective-permute-start.6) | collective-permute-done | bytes 2097184 | tf_op jit(solution)/shard_map/ppermute | solution.py:33
  499.2 80.6 %reduce-scatter.2.cloned.1.call-done = f32[512,512]{0,1:T(8,128)} async-done(((f32[4096,512]{0,1:T(8,128)}), f32[512,512]{0,1:T(8,128)}) %reduce-scatter.2.cloned.1.call-update) | async-done | bytes 1048592 | tf_op jit(solution)/shard_map/reduce_scatter | solution.py:178
  585.2 33.2 %all-gather.6.cloned.1.call-done = bf16[4096,512]{1,0:T(8,128)(2,1)} async-done(((bf16[512,512]{1,0:T(8,128)(2,1)}), bf16[4096,512]{1,0:T(8,128)(2,1)}) %all-gather.6.cloned.1.call-update) | async-done | bytes 4194320 | tf_op jit(solution)/shard_map/all_gather | solution.py:174
  623.3 77.5 %all-gather.8.cloned.1.call-done = f32[2048,512]{0,1:T(8,128)} async-done(((f32[512,512]{0,1:T(8,128)}), f32[2048,512]{0,1:T(8,128)}) %all-gather.8.cloned.1.call-update) | async-done | bytes 4194320 | tf_op jit(solution)/shard_map/all_gather | solution.py:184
  700.7 6.1 reshape.60
  (176 shorter events, 166.1 us)
Async XLA Ops:
  7.2 486.7 %copy-start = (bf16[1,256,4096]{2,1,0:T(8,128)(2,1)S(1)}, bf16[1,256,4096]{2,1,0:T(8,128)(2,1)}, u32[]{:S(2)}) copy-start(bf16[1,256,4096]{2,1,0:T(8,128)(2,1)} %param.12) | copy-start | bytes 6291460
  7.2 54.1 %copy-start.8 = (u32[32]{0:T(128)S(1)}, u32[32]{0:T(128)}, u32[]{:S(2)}) copy-start(u32[32]{0:T(128)} %constant.82) | copy-start | bytes 388
  7.2 51.4 %copy-start.7 = (s32[1,256]{1,0:T(1,128)S(1)}, s32[1,256]{1,0:T(1,128)}, u32[]{:S(2)}) copy-start(s32[1,256]{1,0:T(1,128)} %param.19) | copy-start | bytes 3076
  7.2 572.7 %reduce-scatter.2.cloned.1.call-start = ((), (), s32[]{:S(2)}) async-start(), calls=%async_computation.2 | async-start | bytes 9437184 | tf_op jit(solution)/shard_map/reduce_scatter | solution.py:178
  10.4 4.1 collective-permute-start.1
  14.6 33.3 %collective-permute-start.2 = (bf16[2,512,512]{1,2,0:T(8,128)(2,1)S(1)}, bf16[2,512,512]{1,2,0:T(8,128)(2,1)S(1)}, u32[]{:S(2)}, u32[]{:S(2)}) collective-permute-start(bf16[2,512,512]{1,2,0:T(8,128)(2,1)S(1)} %maximum_maximum_fusion.1), channel_id=1, source_target_pairs={{0,2},{1,3},{2,4},{3,5},{4,6},{5,7},{8,10},{9,11},{10,12},{11,13},... | collective-permute-start | bytes 3145736 | tf_op jit(solution)/shard_map/ppermute | solution.py:33
  50.5 123.1 %collective-permute-start.3 = (bf16[2,1024,512]{1,2,0:T(8,128)(2,1)}, bf16[2,1024,512]{1,2,0:T(8,128)(2,1)}, u32[]{:S(2)}, u32[]{:S(2)}) collective-permute-start(bf16[2,1024,512]{1,2,0:T(8,128)(2,1)} %maximum_maximum_fusion), channel_id=1, source_target_pairs={{0,4},{1,5},{2,6},{3,7},{8,12},{9,13},{10,14},{11,15},{16,20},{17,... | collective-permute-start | bytes 6291464 | tf_op jit(solution)/shard_map/ppermute | solution.py:33
  57.1 115.3 %collective-permute-start = (bf16[2,256,512]{1,2,0:T(8,128)(2,1)}, bf16[2,256,512]{1,2,0:T(8,128)(2,1)}, u32[]{:S(2)}, u32[]{:S(2)}) collective-permute-start(bf16[2,256,512]{1,2,0:T(8,128)(2,1)} %pad_maximum_fusion.1), channel_id=1, source_target_pairs={} | collective-permute-start | bytes 1572872 | tf_op jit(solution)/shard_map/ppermute | solution.py:33
  172.4 3.0 copy-start.3
  194.8 3.5 copy-start.5
  200.9 1.0 copy-start.6
  225.0 3.5 copy-start.5
  231.0 1.0 copy-start.6
  255.1 3.6 copy-start.5
  285.3 3.5 copy-start.5
  310.4 11.8 %slice-start = ((s8[4718592]{0:T(1024)(128)(4,1)}), s8[524288]{0:T(1024)(128)(4,1)S(1)}, s32[]{:S(2)}) async-start(s8[4718592]{0:T(1024)(128)(4,1)} %bitcast.172), calls=%async_computation.4 | async-start | bytes 1048576
  317.1 5.2 slice-start.1
  344.7 6.6 copy-start.1
  347.5 91.6 %collective-permute-start.5 = (f32[2,1024,512]{2,1,0:T(8,128)S(1)}, f32[2,1024,512]{2,1,0:T(8,128)}, u32[]{:S(2)}, u32[]{:S(2)}) collective-permute-start(f32[2,1024,512]{2,1,0:T(8,128)S(1)} %slice.82), channel_id=1, source_target_pairs={{4,0},{5,1},{6,2},{7,3},{12,8},{13,9},{14,10},{15,11},{20,16},{21,... | collective-permute-start | bytes 12582920 | tf_op jit(solution)/shard_map/ppermute | solution.py:33
  350.4 1.8 collective-permute-start.4
  442.5 45.3 %collective-permute-start.6 = (f32[2,512,512]{2,1,0:T(8,128)S(1)}, f32[2,512,512]{2,1,0:T(8,128)S(1)}, u32[]{:S(2)}, u32[]{:S(2)}) collective-permute-start(f32[2,512,512]{2,1,0:T(8,128)S(1)} %slice.84), channel_id=1, source_target_pairs={{2,0},{3,1},{4,2},{5,3},{6,4},{7,5},{10,8},{11,9},{12,10},{13,11},... | collective-permute-start | bytes 6291464 | tf_op jit(solution)/shard_map/ppermute | solution.py:33
  488.3 4.6 collective-permute-start.7
  498.4 120.0 %all-gather.6.cloned.1.call-start = ((), (), s32[]{:S(2)}) async-start(), calls=%async_computation.1 | async-start | bytes 4718592 | tf_op jit(solution)/shard_map/all_gather | solution.py:174
  499.2 201.6 %all-gather.8.cloned.1.call-start = ((), (), s32[]{:S(2)}) async-start(), calls=%async_computation.3 | async-start | bytes 5242880 | tf_op jit(solution)/shard_map/all_gather | solution.py:184
  (4 other events, 3.7 us)
Sparse Core Ops, SparseCore 0:
  498.5 81.2 reduce-scatter.1
  581.8 36.5 all-gather.5
  620.0 80.7 all-gather.7
